TPU v7x, 32 devices: a whole 2x2x4 slice. The times are simulated.
32 devices in a mesh: frame: 4 (over y, x), height: 2 (over core), width: 4 (over z).
Axes of the slice: x: 2, y: 2, z: 4, core: 2. Of those that a mesh axis runs over, the one named last changes fastest.
Arguments:
- tokens: bfloat16 [4, 16, 8, 16, 1536], P('frame', None, 'height', 'width'), may hold values from -6 to 6
- qkv_weight: bfloat16 [3, 768, 1536], P(None, ('frame', 'height')), may hold values from -0.15625 to 0.15625
- tile_mask: int32 [4, 4, 2, 4], P('frame'), may hold values 0 or 1
Outputs:
- attended: bfloat16 [4, 16, 8, 16, 768], P('frame', None, 'height', 'width')
Inputs may be any that keep to these rules, and one draw needn't show every extreme that they name: `tile_mask`: selection flag of each tile.
All inputs are finite; a program needn't handle non-finite values. No bound on the sum of `tile_mask` on one device may be relied on, other than what follows from the above.
Results may differ from a plain program's by a relative error of at most 0.0082.
Values may be sent and summed in bfloat16 or wider, within the bound.
A program may use at most 64 MiB of HBM per device.

v0:
```python
import jax
import jax.numpy as jnp
from jax import lax
from jax.sharding import PartitionSpec as P

HEADS = 6
HEAD_DIM = 128
TILE = 4


epsilon = 1e-06


def padded(block, sides, width):
    for axis, dim in sides:
        count = lax.axis_size(axis)
        forward = [(i, i + 1) for i in range(count - 1)]
        backward = [(target, source) for source, target in forward]
        low = lax.ppermute(
            lax.slice_in_dim(block, block.shape[dim] - width, None, axis=dim), axis, forward
        )
        high = lax.ppermute(lax.slice_in_dim(block, 0, width, axis=dim), axis, backward)
        block = jnp.concatenate([low, block, high], axis=dim)
    return block


def attend(query_part, key_rows_head, value_rows_head, allowed):
    scores = jnp.dot(query_part, key_rows_head.T, preferred_element_type=jnp.float32)
    scores = scores * query_part.shape[-1] ** (-0.5)
    weight = jnp.where(allowed, jnp.exp(scores), jnp.float32(0.0))
    denominator = jnp.sum(weight, -1)
    combined = jnp.dot(
        weight.astype(jnp.bfloat16), value_rows_head, preferred_element_type=jnp.float32
    )
    return combined / denominator[:, None]


def per_device(tokens, qkv_weight, tile_mask):
    clip_count, frames, rows, columns, features = tokens.shape
    token_count = frames * rows * columns
    frame_tiles = frames // TILE
    cube = TILE * TILE * TILE
    token_rows = tokens.reshape(token_count, features).astype(jnp.float32)
    normed = (
        token_rows * lax.rsqrt(jnp.mean(token_rows * token_rows, -1, keepdims=True) + epsilon)
    ).astype(jnp.bfloat16)
    raw = jnp.einsum(
        "td,srd->str",
        normed,
        lax.all_gather(qkv_weight, ("frame", "height"), axis=1, tiled=True),
        preferred_element_type=jnp.float32,
    )
    head_view = raw[:2].reshape(2, token_count, HEADS, HEAD_DIM)
    scaled = head_view * lax.rsqrt(jnp.mean(head_view * head_view, -1, keepdims=True) + epsilon)
    scaled = scaled.reshape(2, token_count, HEADS * HEAD_DIM).astype(jnp.bfloat16)
    query_rows = scaled[0]
    key_rows = scaled[1]
    value_rows = raw[2].astype(jnp.bfloat16)
    clip_mask = jnp.pad(tile_mask[0], 1)
    one_index = jnp.ones((), jnp.int32)
    key_window = lax.dynamic_slice(
        clip_mask,
        (one_index, lax.axis_index("height"), lax.axis_index("width")),
        (frame_tiles, 3, 3),
    )
    key_flags = jnp.broadcast_to(
        key_window[:, None, :, None, :, None] == 1, (frame_tiles, TILE, 3, TILE, 3, TILE)
    )
    key_flags = key_flags.reshape(frames * 9 * TILE * TILE)
    key_count = frames * 9 * TILE * TILE
    key_index = jnp.arange(key_count, dtype=jnp.int32)
    key_tile = key_index // (9 * cube)
    in_frame = key_index % (9 * TILE * TILE)
    centre = (in_frame // (3 * TILE) // TILE == 1) & (in_frame % (3 * TILE) // TILE == 1)
    query_tile = jnp.arange(token_count, dtype=jnp.int32) // cube
    same_tile = query_tile[:, None] == key_tile[None, :]
    near_tile = jnp.abs(query_tile[:, None] - key_tile[None, :]) <= 1
    allowed = near_tile & (key_flags[None, :] | same_tile & centre[None, :])
    results = []
    whole_block = jnp.concatenate([key_rows, value_rows], 1).reshape(
        frames, rows, columns, 2 * HEADS * HEAD_DIM
    )
    extended_all = padded(whole_block, (("height", 1), ("width", 2)), TILE)
    extended_all = extended_all.reshape(key_count, 2 * HEADS * HEAD_DIM)
    value_start = HEADS * HEAD_DIM
    for head_index in range(HEADS):
        low = head_index * HEAD_DIM
        high = low + HEAD_DIM
        results.append(
            attend(
                query_rows[:, low:high],
                extended_all[:, low:high],
                extended_all[:, value_start + low : value_start + high],
                allowed,
            )
        )
    attended = jnp.concatenate(results, 1).astype(jnp.bfloat16)
    return attended.reshape(clip_count, frames, rows, columns, HEADS * HEAD_DIM)


def solution(mesh):
    in_specs = (
        P("frame", None, "height", "width", None),
        P(None, ("frame", "height"), None),
        P("frame", None, None, None),
    )
    out_specs = P("frame", None, "height", "width", None)
    return jax.shard_map(
        per_device, mesh=mesh, in_specs=in_specs, out_specs=out_specs, check_vma=False
    )
```

profile of v0, /device:TPU:0, one launch (start us, length us, event | category | flops | bytes accessed | tf_op | source)
XLA Modules:
  0.0 182.5 jit_solution(12647473184190330011)
XLA Ops:
  6.5 0.7 all-gather.2.cloned.1.call-update
  7.3 1.5 reshape.219
  8.8 0.5 multiply_reduce_fusion
  9.4 51.3 %all-gather.2.cloned.1.call-done = bf16[3,768,1536]{2,1,0:T(8,128)(2,1)} async-done(((bf16[3,96,1536]{2,1,0:T(8,128)(2,1)}), bf16[3,768,1536]{2,1,0:T(8,128)(2,1)}) %all-gather.2.cloned.1.call-update) | async-done | bytes 7077904 | tf_op jit(solution)/shard_map/all_gather | solution.py:50
  60.7 5.1 %convolution_bitcast_fusion = f32[3,256,768]{2,1,0:T(8,128)S(1)} fusion(bf16[3,768,1536]{2,1,0:T(8,128)(2,1)} %all-gather.2.cloned.1.call-done, f32[256,1536]{1,0:T(8,128)S(1)} %reshape.219, f32[256]{0:T(256)S(1)} %rsqrt.20), kind=kOutput, calls=%fused_computation.22 | convolution fusion | flops 1812725760 | bytes 11011072 | tf_op jit(solution)/shard_map/td,srd->str/dot_general | solution.py:47
  66.0 1.3 copy-done.1
  67.3 0.5 copy.4
  68.0 0.5 copy.5
  68.5 1.6 multiply_convert_fusion
  70.7 2.2 %collective-permute-start = (bf16[16,4,4,1536]{3,2,1,0:T(4,128)(2,1)S(1)}, bf16[16,4,4,1536]{3,2,1,0:T(4,128)(2,1)S(1)}, u32[]{:S(2)}, u32[]{:S(2)}) collective-permute-start(bf16[16,4,4,1536]{3,2,1,0:T(4,128)(2,1)S(1)} %constant_dynamic-update-slice_fusion), channel_id=1, source_target_pairs={{0,4},{1,5},{2,6},{3,7},{8,12},{9,13},{10,14},{11,15},{16,20},{17,... | collective-permute-start | bytes 2359304 | tf_op jit(solution)/shard_map/ppermute | solution.py:19
  72.9 1.3 collective-permute-start.1
  74.2 0.5 collective-permute-done
  74.8 2.3 %collective-permute-done.1 = bf16[16,4,4,1536]{3,2,1,0:T(4,128)(2,1)S(1)} collective-permute-done((bf16[16,4,4,1536]{3,2,1,0:T(4,128)(2,1)S(1)}, bf16[16,4,4,1536]{3,2,1,0:T(4,128)(2,1)S(1)}, u32[]{:S(2)}, u32[]{:S(2)}) %collective-permute-start.1) | collective-permute-done | bytes 786464 | tf_op jit(solution)/shard_map/ppermute | solution.py:22
  77.1 2.7 %pad_maximum_fusion.1 = bf16[16,12,4,1536]{3,2,1,0:T(4,128)(2,1)} fusion(bf16[16,4,4,1536]{3,2,1,0:T(4,128)(2,1)S(1)} %collective-permute-done.1, bf16[16,4,4,1536]{3,2,1,0:T(4,128)(2,1)S(1)} %constant_dynamic-update-slice_fusion, bf16[16,4,4,1536]{3,2,1,0:T(4,128)(2,1)S(1)} %collective-permute-done), kind=kLoop, calls=%fused_computation.19 | loop fusion | flops 2359296 | bytes 4718592 | tf_op jit(solution)/shard_map/concatenate | solution.py:23
  79.8 4.9 %collective-permute-start.2 = (bf16[16,12,4,1536]{3,2,1,0:T(4,128)(2,1)}, bf16[16,12,4,1536]{3,2,1,0:T(4,128)(2,1)}, u32[]{:S(2)}, u32[]{:S(2)}) collective-permute-start(bf16[16,12,4,1536]{3,2,1,0:T(4,128)(2,1)} %pad_maximum_fusion.1), channel_id=1, source_target_pairs={{0,1},{1,2},{2,3},{4,5},{5,6},{6,7},{8,9},{9,10},{10,11},{12,13},{... | collective-permute-start | bytes 7077896 | tf_op jit(solution)/shard_map/ppermute | solution.py:19
  84.7 1.3 collective-permute-start.3
  86.5 47.8 %collective-permute-done.2 = bf16[16,12,4,1536]{3,2,1,0:T(4,128)(2,1)} collective-permute-done((bf16[16,12,4,1536]{3,2,1,0:T(4,128)(2,1)}, bf16[16,12,4,1536]{3,2,1,0:T(4,128)(2,1)}, u32[]{:S(2)}, u32[]{:S(2)}) %collective-permute-start.2) | collective-permute-done | bytes 2359328 | tf_op jit(solution)/shard_map/ppermute | solution.py:19
  134.3 5.6 %collective-permute-done.3 = bf16[16,12,4,1536]{3,2,1,0:T(4,128)(2,1)} collective-permute-done((bf16[16,12,4,1536]{3,2,1,0:T(4,128)(2,1)}, bf16[16,12,4,1536]{3,2,1,0:T(4,128)(2,1)}, u32[]{:S(2)}, u32[]{:S(2)}) %collective-permute-start.3) | collective-permute-done | bytes 2359328 | tf_op jit(solution)/shard_map/ppermute | solution.py:22
  139.9 8.7 %pad_maximum_fusion = bf16[16,12,12,1536]{3,2,1,0:T(8,128)(2,1)} fusion(bf16[16,12,4,1536]{3,2,1,0:T(4,128)(2,1)} %collective-permute-done.3, bf16[16,4,4,1536]{3,2,1,0:T(4,128)(2,1)S(1)} %collective-permute-done.1, bf16[16,4,4,1536]{3,2,1,0:T(4,128)(2,1)S(1)} %constant_dynamic-update-slice_fusion, bf16[16,4,4,1536]{3,2,1,0:T(4,128)(2,1)S(1)} %collective-permute-done, ...), kind=kLoop, calls=%fused_computation | loop fusion | flops 35389440 | bytes 14155776 | tf_op jit(solution)/shard_map/concatenate | solution.py:23
  148.6 11.5 %reshape.218 = bf16[2304,1536]{1,0:T(8,128)(2,1)} reshape(bf16[16,12,12,1536]{3,2,1,0:T(8,128)(2,1)} %pad_maximum_fusion) | data formatting | bytes 14155776 | tf_op jit(solution)/shard_map/reshape | solution.py:84
  160.1 2.8 %fusion.106 = (f32[256]{0:T(256)S(1)}, bf16[256,2304]{1,0:T(8,128)(2,1)S(1)}) fusion(bf16[2304,1536]{1,0:T(8,128)(2,1)} %reshape.218, bf16[256,768]{1,0:T(8,128)(2,1)S(1)} %get-tuple-element.5, pred[2304]{0:T(1024)(128)(4,1)S(1)} %fusion.99, pred[2304]{0:T(1024)(128)(4,1)S(1)} %or.10, s32[2304]{0:T(1024)S(1)} %add_select_fusion.5, s32[256]{0:T(256)S(1)} %and_select_fusion), kind=kOutput, calls=%fused_computation.131 | convolution fusion | flops 157482752 | bytes 1855488 | tf_op jit(solution)/shard_map/dot_general | solution.py:28
  163.3 1.6 fusion.105
  164.8 1.6 fusion.104
  166.4 1.6 fusion.103
  168.0 1.6 fusion.102
  169.6 1.6 fusion.101
  171.2 0.5 fusion.58
  171.7 0.5 fusion.43
  172.6 0.5 fusion.49
  173.5 0.5 fusion.55
  174.2 0.7 copy-done.3
  175.0 0.7 constant_dynamic-update-slice_fusion.2
  (34 shorter events, 3.1 us)
Async XLA Ops:
  6.5 2.2 %copy-start.2 = (bf16[1,16,4,4,1536]{4,3,2,1,0:T(4,128)(2,1)S(1)}, bf16[1,16,4,4,1536]{4,3,2,1,0:T(4,128)(2,1)}, u32[]{:S(2)}) copy-start(bf16[1,16,4,4,1536]{4,3,2,1,0:T(4,128)(2,1)} %param.3) | copy-start | bytes 2359300
  6.5 54.2 %all-gather.2.cloned.1.call-start = ((), (), s32[]{:S(2)}) async-start(), calls=%async_computation | async-start | bytes 7962624 | tf_op jit(solution)/shard_map/all_gather | solution.py:50
  65.8 1.4 copy-start.1
  70.7 15.3 %copy-start.4 = (s32[1,4,2,4]{3,2,1,0:T(2,128)S(1)}, s32[1,4,2,4]{3,2,1,0:T(2,128)}, u32[]{:S(2)}) copy-start(s32[1,4,2,4]{3,2,1,0:T(2,128)} %param.5) | copy-start | bytes 388
  70.7 4.1 %collective-permute-start = (bf16[16,4,4,1536]{3,2,1,0:T(4,128)(2,1)S(1)}, bf16[16,4,4,1536]{3,2,1,0:T(4,128)(2,1)S(1)}, u32[]{:S(2)}, u32[]{:S(2)}) collective-permute-start(bf16[16,4,4,1536]{3,2,1,0:T(4,128)(2,1)S(1)} %constant_dynamic-update-slice_fusion), channel_id=1, source_target_pairs={{0,4},{1,5},{2,6},{3,7},{8,12},{9,13},{10,14},{11,15},{16,20},{17,... | collective-permute-start | bytes 2359304 | tf_op jit(solution)/shard_map/ppermute | solution.py:19
  72.9 4.2 %collective-permute-start.1 = (bf16[16,4,4,1536]{3,2,1,0:T(4,128)(2,1)S(1)}, bf16[16,4,4,1536]{3,2,1,0:T(4,128)(2,1)S(1)}, u32[]{:S(2)}, u32[]{:S(2)}) collective-permute-start(bf16[16,4,4,1536]{3,2,1,0:T(4,128)(2,1)S(1)} %constant_dynamic-update-slice_fusion), channel_id=1, source_target_pairs={{4,0},{5,1},{6,2},{7,3},{12,8},{13,9},{14,10},{15,11},{20,16},{21,... | collective-permute-start | bytes 2359304 | tf_op jit(solution)/shard_map/ppermute | solution.py:22
  79.8 54.5 %collective-permute-start.2 = (bf16[16,12,4,1536]{3,2,1,0:T(4,128)(2,1)}, bf16[16,12,4,1536]{3,2,1,0:T(4,128)(2,1)}, u32[]{:S(2)}, u32[]{:S(2)}) collective-permute-start(bf16[16,12,4,1536]{3,2,1,0:T(4,128)(2,1)} %pad_maximum_fusion.1), channel_id=1, source_target_pairs={{0,1},{1,2},{2,3},{4,5},{5,6},{6,7},{8,9},{9,10},{10,11},{12,13},{... | collective-permute-start | bytes 7077896 | tf_op jit(solution)/shard_map/ppermute | solution.py:19
  84.7 55.2 %collective-permute-start.3 = (bf16[16,12,4,1536]{3,2,1,0:T(4,128)(2,1)}, bf16[16,12,4,1536]{3,2,1,0:T(4,128)(2,1)}, u32[]{:S(2)}, u32[]{:S(2)}) collective-permute-start(bf16[16,12,4,1536]{3,2,1,0:T(4,128)(2,1)} %pad_maximum_fusion.1), channel_id=1, source_target_pairs={{1,0},{2,1},{3,2},{5,4},{6,5},{7,6},{9,8},{10,9},{11,10},{13,12},{... | collective-permute-start | bytes 7077896 | tf_op jit(solution)/shard_map/ppermute | solution.py:22
  160.1 3.2 %copy-start = (bf16[2304,1536]{1,0:T(8,128)(2,1)S(1)}, bf16[2304,1536]{1,0:T(8,128)(2,1)}, u32[]{:S(2)}) copy-start(bf16[2304,1536]{1,0:T(8,128)(2,1)} %reshape.218) | copy-start | bytes 21233668
  174.2 0.7 copy-start.3
Sparse Core Ops, SparseCore 0:
  9.2 51.4 all-gather.1
where the time goes:
time: 183 us; the launch traced here: 182 us
  waiting for transfers between devices  108 us (59%)
  matrix products  18.6 us (10%)
  local copies, waits for them, and re-layouts  18.4 us (10%)
  other arithmetic  13.9 us (8%)
  between operations  13.7 us (7%)
  starting transfers between devices  9.67 us (5%)
    all_gather x1, waiting for transfers between devices, per_device(): lax.all_gather(qkv_weight, ('frame', 'height'), axis=1, tiled=True)  51.3 us
    ppermute x2, waiting for transfers between devices, padded(): lax.ppermute(lax.slice_in_dim(block, block.shape[dim] - width, None, axis...  48.3 us
    reshape x1, local copies, waits for them, and re-layouts, per_device(): extended_all = extended_all.reshape(key_count, 2 * HEADS * HEAD_DIM)  11.5 us
    concatenate x2, other arithmetic, padded(): block = jnp.concatenate([low, block, high], axis=dim)  11.4 us
    dot_general x6, matrix products, attend(): jnp.dot(query_part, key_rows_head.T, preferred_element_type=jnp.float32)  10.7 us
    ppermute x2, waiting for transfers between devices, padded(): lax.ppermute(lax.slice_in_dim(block, 0, width, axis=dim), axis, backward)  7.94 us
    ppermute x2, starting transfers between devices, padded(): lax.ppermute(lax.slice_in_dim(block, block.shape[dim] - width, None, axis...  7.1 us
    dot_general x1, matrix products, per_device(): jnp.einsum('td,srd->str', normed, lax.all_gather(qkv_weight, ('frame', 'h...  5.11 us
  transfers between devices with their start and end apart: 5, of which 5 were waited for; matrix products, arithmetic and copies ran while one was open for 1% of the time, Pallas kernels for 0%

commit v1 on v0

v1 whole, which is shorter than its diff:
```python
import functools
import math

import jax
import jax.numpy as jnp
from jax import lax
from jax.experimental import pallas as pl
from jax.experimental.pallas import tpu as pltpu
from jax.sharding import PartitionSpec as P

HEAD_DIM = 128
TILE = 4
CUBE = TILE * TILE * TILE
MESH = pl.DeviceIdType.MESH

epsilon = 1e-06


def kernel(
    n_h, n_w, x_ref, w_ref, tm_ref, o_ref,
    xs, xn, w_all, kbuf, vbuf, qbuf, mask,
    loc_sem, tok_s, tok_r, own_s, own_r, fwd_s, fwd_r, hgt_s, hgt_r, kvx_s, kvx_r,
):
    f, h, w = lax.axis_index("frame"), lax.axis_index("height"), lax.axis_index("width")
    f1 = f + 1 - 2 * (f % 2)
    f2 = f + 2 - 4 * ((f // 2) % 2)
    rows = w_ref.shape[1]
    features = w_ref.shape[2]
    half = features // 2
    tokens = xn.shape[0] // 3
    heads = kbuf.shape[2]
    slots = kbuf.shape[1]
    key, value, query = 1, 2, 0

    def row(parity, height):
        return pl.ds(pl.multiple_of((parity * n_h + height) * rows, rows), rows)

    parity = f % 2
    mine, beside = row(parity, h), row(1 - parity, h)

    def remote(src, dst, send, recv, target):
        return pltpu.make_async_remote_copy(
            src_ref=src, dst_ref=dst, send_sem=send, recv_sem=recv,
            device_id=target, device_id_type=MESH,
        )

    def to_frame(i):
        return ((f1, f2)[i], h, w)

    def own_copy(s, i):
        return remote(w_ref.at[s], w_all.at[s, i, mine], own_s.at[s, i], own_r.at[s, i], to_frame(i))

    def fwd_copy(s, i):
        cols = pl.ds(0, half) if i == 1 else pl.ds(half, half)
        src = w_all.at[s, 0, beside, cols] if i == 1 else w_all.at[s, 1, mine, cols]
        dst = w_all.at[s, 1, beside if i == 1 else mine, cols]
        return remote(src, dst, fwd_s.at[s, i], fwd_r.at[s, i], to_frame(i))

    piece_at = ((0, mine), (0, beside), (1, mine), (1, beside))

    def hgt_copy(s, piece, d):
        group, place = piece_at[piece]
        dst = w_all.at[s, group, place]
        src = w_ref.at[s] if piece == 0 else dst
        target = (f, lax.rem(h + d, n_h), w)
        return remote(src, dst, hgt_s.at[s, piece, d - 1], hgt_r.at[s, piece, d - 1], target)

    def kv_copy(g, which, up):
        buf = (kbuf, vbuf)[which]
        slot = 1 if up or n_h == 2 else 2
        target = (f, h + 1 if up else h - 1, w)
        e = 0 if up else 1
        return remote(buf.at[g, 0], buf.at[g, slot], kvx_s.at[g, which, e], kvx_r.at[g, which, e], target)

    def tok_copy(e):
        target = (f, h, w + 1 if e == 0 else w - 1)
        return remote(x_ref.at[0], xs.at[0 if e == 0 else 2], tok_s.at[e], tok_r.at[e], target)

    local_x = pltpu.make_async_copy(x_ref.at[0], xs.at[1], loc_sem.at[0])
    local_w = [
        pltpu.make_async_copy(w_ref.at[s], w_all.at[s, 0, mine], loc_sem.at[1 + s]) for s in range(3)
    ]
    local_x.start()
    for s in range(3):
        local_w[s].start()

    has_left, has_right = w > 0, w < n_w - 1
    has_below, has_above = h > 0, h < n_h - 1

    barrier = pltpu.get_barrier_semaphore()

    def greet(target):
        pl.semaphore_signal(barrier, inc=1, device_id=target, device_id_type=MESH)

    greet(to_frame(0))
    greet(to_frame(1))
    for d in range(1, n_h):
        greet((f, lax.rem(h + d, n_h), w))

    @pl.when(has_left)
    def _():
        greet((f, h, w - 1))

    @pl.when(has_right)
    def _():
        greet((f, h, w + 1))

    peers = n_h + 1 + has_left.astype(jnp.int32) + has_right.astype(jnp.int32)
    pl.semaphore_wait(barrier, peers)

    for s in (key, value, query):
        own_copy(s, 0).start()
        own_copy(s, 1).start()
        if s == key:
            @pl.when(has_right)
            def _():
                tok_copy(0).start()

            @pl.when(has_left)
            def _():
                tok_copy(1).start()
        for d in range(1, n_h):
            hgt_copy(s, 0, d).start()

    q_tile = lax.broadcasted_iota(jnp.int32, (tokens, tokens), 0) // CUBE
    k_tile = lax.broadcasted_iota(jnp.int32, (tokens, tokens), 1) // CUBE
    near = jnp.abs(q_tile - k_tile) <= 1
    same = q_tile == k_tile
    total_h, total_w = tm_ref.shape[2], tm_ref.shape[3]
    for b in range(slots):
        if b == 0:
            row_h = h
        elif n_h == 2:
            row_h = 1 - h
        else:
            row_h = h - 1 if b == 1 else h + 1
        for c in range(3):
            col_w = w + c - 1
            inside = ((row_h >= 0) & (row_h < total_h) & (col_w >= 0) & (col_w < total_w)).astype(jnp.int32)
            at_h = jnp.minimum(jnp.maximum(row_h, 0), total_h - 1)
            at_w = jnp.minimum(jnp.maximum(col_w, 0), total_w - 1)
            flags = jnp.zeros((tokens, tokens), jnp.int32)
            for t in range(tokens // CUBE):
                flag = tm_ref[0, t, at_h, at_w] * inside
                flags = jnp.where(k_tile == t, flag, flags)
            seen = flags == 1
            if b == 0 and c == 1:
                seen = seen | same
            allowed = jnp.where(near & seen, jnp.float32(1.0), jnp.float32(0.0))
            mask[b, :, c * tokens : (c + 1) * tokens] = allowed.astype(jnp.bfloat16)

    def normalise(c):
        step = 64
        for t in range(tokens // step):
            frames = step // (TILE * TILE)
            block = xs[c, t * frames : (t + 1) * frames].astype(jnp.float32).reshape(step, features)
            scale = lax.rsqrt(jnp.mean(block * block, -1, keepdims=True) + epsilon)
            xn[c * tokens + t * step : c * tokens + (t + 1) * step, :] = (block * scale).astype(jnp.bfloat16)

    def blank(c):
        xn[c * tokens : (c + 1) * tokens, :] = jnp.zeros((tokens, features), jnp.bfloat16)

    local_x.wait()
    normalise(1)

    def relay(s):
        own_copy(s, 0).wait_recv()
        fwd_copy(s, 1).start()
        for d in range(1, n_h):
            hgt_copy(s, 1, d).start()
        own_copy(s, 1).wait_recv()
        fwd_copy(s, 0).start()
        for d in range(1, n_h):
            hgt_copy(s, 2, d).start()

    def head_norm(raw):
        return (raw * lax.rsqrt(jnp.mean(raw * raw, -1, keepdims=True) + epsilon)).astype(jnp.bfloat16)

    contract_last = (((1,), (1,)), ((), ()))

    def project_kv(g, s):
        buf = kbuf if s == key else vbuf

        def body(c, carry):
            at = pl.ds(pl.multiple_of(c * tokens, tokens), tokens)
            raw = lax.dot_general(xn[at, :], w_all[s, g], contract_last, preferred_element_type=jnp.float32)
            for j in range(heads):
                part = raw[:, j * HEAD_DIM : (j + 1) * HEAD_DIM]
                buf[g, 0, j, at, :] = head_norm(part) if s == key else part.astype(jnp.bfloat16)
            return carry

        lax.fori_loop(0, 3, body, 0)
        which = 0 if s == key else 1

        @pl.when(has_above)
        def _():
            kv_copy(g, which, True).start()

        @pl.when(has_below)
        def _():
            kv_copy(g, which, False).start()

    def project_q(g):
        raw = lax.dot_general(
            xn[tokens : 2 * tokens, :], w_all[query, g], contract_last, preferred_element_type=jnp.float32
        )
        for j in range(heads):
            qbuf[g, j] = head_norm(raw[:, j * HEAD_DIM : (j + 1) * HEAD_DIM])

    def wait_kv(g):
        for which in range(2):
            @pl.when(has_below)
            def _():
                kv_copy(g, which, True).wait_recv()

            @pl.when(has_above)
            def _():
                kv_copy(g, which, False).wait_recv()

    def wait_hgt(s, pieces):
        for piece in pieces:
            for d in range(1, n_h):
                hgt_copy(s, piece, d).wait_recv()

    factor = HEAD_DIM ** (-0.5) * math.log2(math.e)
    ones = jnp.ones((3 * tokens, HEAD_DIM), jnp.bfloat16)

    def attend(g):
        pair = f // 2
        base = (pair if g == 0 else 1 - pair) * heads

        def body(j, carry):
            q = qbuf[g, j]
            total = jnp.zeros((tokens, 2 * HEAD_DIM), jnp.float32)
            for b in range(slots):
                scores = lax.dot_general(q, kbuf[g, b, j], contract_last, preferred_element_type=jnp.float32)
                weight = jnp.exp2(scores * factor).astype(jnp.bfloat16) * mask[b]
                wide = jnp.concatenate([vbuf[g, b, j], ones], 1)
                total = total + jnp.dot(weight, wide, preferred_element_type=jnp.float32)
            result = (total[:, :HEAD_DIM] / total[:, HEAD_DIM:]).astype(o_ref.dtype)
            lanes = pl.ds(pl.multiple_of((base + j) * HEAD_DIM, HEAD_DIM), HEAD_DIM)
            o_ref[:, lanes] = result
            return carry

        lax.fori_loop(0, heads, body, 0)

    if n_h > 2:
        for edge, slot in ((h == 0, 1), (h == n_h - 1, 2)):
            @pl.when(edge)
            def _():
                for g in range(2):
                    kbuf[g, slot] = jnp.zeros(kbuf.shape[2:], jnp.bfloat16)
                    vbuf[g, slot] = jnp.zeros(vbuf.shape[2:], jnp.bfloat16)

    relay(key)
    relay(value)

    @pl.when(has_left)
    def _():
        tok_copy(0).wait_recv()
        normalise(0)

    @pl.when(w == 0)
    def _():
        blank(0)

    @pl.when(has_right)
    def _():
        tok_copy(1).wait_recv()
        normalise(2)

    @pl.when(w == n_w - 1)
    def _():
        blank(2)

    for s in (key, value):
        local_w[s].wait()
        wait_hgt(s, (0, 1))
        project_kv(0, s)
    relay(query)
    local_w[query].wait()
    wait_hgt(query, (0, 1))
    project_q(0)
    wait_kv(0)
    attend(0)
    for s in (key, value, query):
        fwd_copy(s, 0).wait_recv()
        fwd_copy(s, 1).wait_recv()
        for d in range(1, n_h):
            hgt_copy(s, 3, d).start()
        wait_hgt(s, (2, 3))
        if s == query:
            project_q(1)
        else:
            project_kv(1, s)
    wait_kv(1)
    attend(1)

    for s in range(3):
        for i in range(2):
            own_copy(s, i).wait_send()
            fwd_copy(s, i).wait_send()
        for piece in range(4):
            for d in range(1, n_h):
                hgt_copy(s, piece, d).wait_send()

    @pl.when(has_right)
    def _():
        tok_copy(0).wait_send()

    @pl.when(has_left)
    def _():
        tok_copy(1).wait_send()

    for g in range(2):
        for which in range(2):
            @pl.when(has_above)
            def _():
                kv_copy(g, which, True).wait_send()

            @pl.when(has_below)
            def _():
                kv_copy(g, which, False).wait_send()


def per_device(n_f, n_h, n_w, tokens, qkv_weight, tile_mask):
    clips, frames, rows, columns, features = tokens.shape
    count = frames * rows * columns
    width = qkv_weight.shape[1] * n_f * n_h
    if n_f != 4 or n_h < 2 or clips != 1 or rows != TILE or columns != TILE:
        raise ValueError("unsupported placement")
    heads = width // HEAD_DIM // 2
    slots = 2 if n_h == 2 else 3
    dma = pltpu.SemaphoreType.DMA
    out = pl.pallas_call(
        functools.partial(kernel, n_h, n_w),
        out_shape=jax.ShapeDtypeStruct((count, width), jnp.bfloat16),
        in_specs=[
            pl.BlockSpec(memory_space=pl.ANY),
            pl.BlockSpec(memory_space=pl.ANY),
            pl.BlockSpec(memory_space=pltpu.SMEM),
        ],
        out_specs=pl.BlockSpec(memory_space=pltpu.VMEM),
        scratch_shapes=[
            pltpu.VMEM((3, frames, rows, columns, features), jnp.bfloat16),
            pltpu.VMEM((3 * count, features), jnp.bfloat16),
            pltpu.VMEM((3, 2, width // 2, features), jnp.bfloat16),
            pltpu.VMEM((2, slots, heads, 3 * count, HEAD_DIM), jnp.bfloat16),
            pltpu.VMEM((2, slots, heads, 3 * count, HEAD_DIM), jnp.bfloat16),
            pltpu.VMEM((2, heads, count, HEAD_DIM), jnp.bfloat16),
            pltpu.VMEM((slots, count, 3 * count), jnp.bfloat16),
            dma((4,)), dma((2,)), dma((2,)), dma((3, 2)), dma((3, 2)), dma((3, 2)), dma((3, 2)),
            dma((3, 4, n_h - 1)), dma((3, 4, n_h - 1)), dma((2, 2, 2)), dma((2, 2, 2)),
        ],
        compiler_params=pltpu.CompilerParams(
            collective_id=0, has_side_effects=True, vmem_limit_bytes=56 << 20
        ),
    )(tokens, qkv_weight, tile_mask)
    return out.reshape(clips, frames, rows, columns, width)


def solution(mesh):
    in_specs = (
        P("frame", None, "height", "width", None),
        P(None, ("frame", "height"), None),
        P("frame", None, None, None),
    )
    out_specs = P("frame", None, "height", "width", None)
    body = functools.partial(
        per_device, mesh.shape["frame"], mesh.shape["height"], mesh.shape["width"]
    )
    return jax.shard_map(body, mesh=mesh, in_specs=in_specs, out_specs=out_specs, check_vma=False)
```

time: 183 us -> 49.1 us (0.27)
  waiting for transfers between devices: 108 us -> 0 us
  Pallas kernels: 0 us -> 47.1 us
  matrix products: 18.6 us -> 0 us
  local copies, waits for them, and re-layouts: 18.4 us -> 1.84 us
  other arithmetic: 13.9 us -> 0 us
  between operations: 13.7 us -> 0.01 us
  starting transfers between devices: 9.67 us -> 0 us
    ppermute x4 -> x0, waiting for transfers between devices: 56.3 us -> none  [the longest x2 48.3 us: padded(): lax.ppermute(lax.slice_in_dim(block, block.shape[dim] - width, None, axis...]
    all_gather x1 -> x0, waiting for transfers between devices: 51.3 us -> none  [per_device(): lax.all_gather(qkv_weight, ('frame', 'height'), axis=1, tiled=True)]
    pallas_call x0 -> x1, Pallas kernels: none -> 47.1 us  [per_device(): pl.pallas_call(functools.partial(kernel, n_h, n_w), out_shape=jax.ShapeDt...]
    dot_general x13 -> x0, matrix products: 18.6 us -> none  [the longest x6 10.7 us: attend(): jnp.dot(query_part, key_rows_head.T, preferred_element_type=jnp.float32)]
    concatenate x2 -> x0, other arithmetic: 11.4 us -> none  [padded(): block = jnp.concatenate([low, block, high], axis=dim)]
    ppermute x4 -> x0, starting transfers between devices: 9.67 us -> none  [the longest x2 7.1 us: padded(): lax.ppermute(lax.slice_in_dim(block, block.shape[dim] - width, None, axis...]
    reshape x1, local copies, waits for them, and re-layouts: 11.5 us -> 1.84 us  [per_device(): return out.reshape(clips, frames, rows, columns, width)]
    unnamed x16 -> x0, local copies, waits for them, and re-layouts: 2.85 us -> none
  transfers between devices with their start and end apart: 5 -> 0, of which waited for: 5 -> 0; matrix products, arithmetic and copies ran while one was open for 1% -> 0% of each run, Pallas kernels for 0% -> 0%
where the time goes in v1:
time: 49.1 us; the launch traced here: 48.9 us
  Pallas kernels  47.1 us (96%)
  local copies, waits for them, and re-layouts  1.84 us (4%)
    pallas_call x1, Pallas kernels, per_device(): pl.pallas_call(functools.partial(kernel, n_h, n_w), out_shape=jax.ShapeDt...  47.1 us
    reshape x1, local copies, waits for them, and re-layouts, per_device(): return out.reshape(clips, frames, rows, columns, width)  1.84 us

profile of v1, /device:TPU:0, one launch (start us, length us, event | category | flops | bytes accessed | tf_op | source)
XLA Modules:
  0.0 48.9 jit_solution(15246846789188721763)
XLA Ops:
  0.0 47.1 %shard_map.37 = bf16[256,768]{1,0:T(8,128)(2,1)} custom-call(bf16[1,16,4,4,1536]{4,3,2,1,0:T(4,128)(2,1)} %x_ref.1, bf16[3,96,1536]{2,1,0:T(8,128)(2,1)} %w_ref.1, s32[1,4,2,4]{3,2,1,0:T(2,128)} %tm_ref.1), custom_call_target="tpu_custom_call" | custom-call | tf_op jit(solution)/shard_map/pallas_call | solution.py:335
  47.1 1.8 %reshape.3 = bf16[1,16,4,4,768]{4,3,2,1,0:T(4,128)(2,1)} reshape(bf16[256,768]{1,0:T(8,128)(2,1)} %shard_map.37) | data formatting | bytes 786432 | tf_op jit(solution)/shard_map/reshape | solution.py:359

commit v2 on v1

--- a/solution.py
+++ b/solution.py
@@ -47,8 +47,11 @@
     def to_frame(i):
         return ((f1, f2)[i], h, w)
 
-    def own_copy(s, i):
-        return remote(w_ref.at[s], w_all.at[s, i, mine], own_s.at[s, i], own_r.at[s, i], to_frame(i))
+    def own_copy(s, p, i):
+        cols = pl.ds(p * half, half)
+        return remote(
+            w_ref.at[s, :, cols], w_all.at[s, i, mine, cols], own_s.at[s, p, i], own_r.at[s, p, i], to_frame(i)
+        )
 
     def fwd_copy(s, i):
         cols = pl.ds(0, half) if i == 1 else pl.ds(half, half)
@@ -108,19 +111,41 @@
     peers = n_h + 1 + has_left.astype(jnp.int32) + has_right.astype(jnp.int32)
     pl.semaphore_wait(barrier, peers)
 
+    def send_own(s, p):
+        own_copy(s, p, 0).start()
+        own_copy(s, p, 1).start()
+
+    def wait_own(s, p):
+        own_copy(s, p, 0).wait_recv()
+        own_copy(s, p, 1).wait_recv()
+
+    def send_fwd(s):
+        fwd_copy(s, 0).start()
+        fwd_copy(s, 1).start()
+
+    def relay(s, *pieces):
+        for piece in pieces:
+            for d in range(1, n_h):
+                hgt_copy(s, piece, d).start()
+
+    def take_fwd(s):
+        fwd_copy(s, 0).wait_recv()
+        fwd_copy(s, 1).wait_recv()
+        relay(s, 3)
+
+    send_own(key, 0)
+    send_own(key, 1)
+
+    @pl.when(has_right)
+    def _():
+        tok_copy(0).start()
+
+    @pl.when(has_left)
+    def _():
+        tok_copy(1).start()
+
     for s in (key, value, query):
-        own_copy(s, 0).start()
-        own_copy(s, 1).start()
-        if s == key:
-            @pl.when(has_right)
-            def _():
-                tok_copy(0).start()
-
-            @pl.when(has_left)
-            def _():
-                tok_copy(1).start()
-        for d in range(1, n_h):
-            hgt_copy(s, 0, d).start()
+        relay(s, 0)
 
     q_tile = lax.broadcasted_iota(jnp.int32, (tokens, tokens), 0) // CUBE
     k_tile = lax.broadcasted_iota(jnp.int32, (tokens, tokens), 1) // CUBE
@@ -160,36 +185,30 @@
     def blank(c):
         xn[c * tokens : (c + 1) * tokens, :] = jnp.zeros((tokens, features), jnp.bfloat16)
 
-    local_x.wait()
-    normalise(1)
-
-    def relay(s):
-        own_copy(s, 0).wait_recv()
-        fwd_copy(s, 1).start()
-        for d in range(1, n_h):
-            hgt_copy(s, 1, d).start()
-        own_copy(s, 1).wait_recv()
-        fwd_copy(s, 0).start()
-        for d in range(1, n_h):
-            hgt_copy(s, 2, d).start()
-
     def head_norm(raw):
         return (raw * lax.rsqrt(jnp.mean(raw * raw, -1, keepdims=True) + epsilon)).astype(jnp.bfloat16)
 
     contract_last = (((1,), (1,)), ((), ()))
 
-    def project_kv(g, s):
+    def project_kv(g, s, sides):
         buf = kbuf if s == key else vbuf
 
-        def body(c, carry):
+        def block(c):
             at = pl.ds(pl.multiple_of(c * tokens, tokens), tokens)
             raw = lax.dot_general(xn[at, :], w_all[s, g], contract_last, preferred_element_type=jnp.float32)
             for j in range(heads):
                 part = raw[:, j * HEAD_DIM : (j + 1) * HEAD_DIM]
                 buf[g, 0, j, at, :] = head_norm(part) if s == key else part.astype(jnp.bfloat16)
+
+        if not sides:
+            block(1)
+            return
+
+        def body(i, carry):
+            block(2 * i)
             return carry
 
-        lax.fori_loop(0, 3, body, 0)
+        lax.fori_loop(0, 2, body, 0)
         which = 0 if s == key else 1
 
         @pl.when(has_above)
@@ -200,12 +219,13 @@
         def _():
             kv_copy(g, which, False).start()
 
-    def project_q(g):
+    def project_q(g, first, count):
+        place = pl.ds(pl.multiple_of(first * HEAD_DIM, HEAD_DIM), count * HEAD_DIM)
         raw = lax.dot_general(
-            xn[tokens : 2 * tokens, :], w_all[query, g], contract_last, preferred_element_type=jnp.float32
+            xn[tokens : 2 * tokens, :], w_all[query, g, place], contract_last, preferred_element_type=jnp.float32
         )
-        for j in range(heads):
-            qbuf[g, j] = head_norm(raw[:, j * HEAD_DIM : (j + 1) * HEAD_DIM])
+        for j in range(count):
+            qbuf[g, first + j] = head_norm(raw[:, j * HEAD_DIM : (j + 1) * HEAD_DIM])
 
     def wait_kv(g):
         for which in range(2):
@@ -225,11 +245,12 @@
     factor = HEAD_DIM ** (-0.5) * math.log2(math.e)
     ones = jnp.ones((3 * tokens, HEAD_DIM), jnp.bfloat16)
 
-    def attend(g):
+    def attend(g, first, count):
         pair = f // 2
         base = (pair if g == 0 else 1 - pair) * heads
 
-        def body(j, carry):
+        def body(i, carry):
+            j = first + i
             q = qbuf[g, j]
             total = jnp.zeros((tokens, 2 * HEAD_DIM), jnp.float32)
             for b in range(slots):
@@ -242,7 +263,7 @@
             o_ref[:, lanes] = result
             return carry
 
-        lax.fori_loop(0, heads, body, 0)
+        lax.fori_loop(0, count, body, 0)
 
     if n_h > 2:
         for edge, slot in ((h == 0, 1), (h == n_h - 1, 2)):
@@ -252,9 +273,26 @@
                     kbuf[g, slot] = jnp.zeros(kbuf.shape[2:], jnp.bfloat16)
                     vbuf[g, slot] = jnp.zeros(vbuf.shape[2:], jnp.bfloat16)
 
-    relay(key)
-    relay(value)
-
+    local_x.wait()
+    normalise(1)
+    wait_own(key, 0)
+    send_own(value, 0)
+    fwd_copy(key, 1).start()
+    wait_own(key, 1)
+    fwd_copy(key, 0).start()
+    relay(key, 1, 2)
+    wait_own(value, 0)
+    send_own(value, 1)
+    local_w[key].wait()
+    wait_hgt(key, (0, 1))
+    project_kv(0, key, False)
+    take_fwd(key)
+    send_own(query, 0)
+    wait_hgt(key, (2, 3))
+    project_kv(1, key, False)
+    wait_own(value, 1)
+    send_own(query, 1)
+    relay(value, 1, 2)
     @pl.when(has_left)
     def _():
         tok_copy(0).wait_recv()
@@ -273,32 +311,40 @@
     def _():
         blank(2)
 
-    for s in (key, value):
-        local_w[s].wait()
-        wait_hgt(s, (0, 1))
-        project_kv(0, s)
-    relay(query)
+    project_kv(0, key, True)
+    wait_own(query, 0)
+    send_fwd(value)
+    local_w[value].wait()
+    wait_hgt(value, (0, 1))
+    project_kv(0, value, False)
+    project_kv(0, value, True)
+    wait_own(query, 1)
+    send_fwd(query)
+    relay(query, 1, 2)
+    project_kv(1, key, True)
+    early = n_h * rows // HEAD_DIM
     local_w[query].wait()
     wait_hgt(query, (0, 1))
-    project_q(0)
+    project_q(0, 0, heads)
+    wait_hgt(query, (2,))
+    project_q(1, parity * (heads - early), early)
     wait_kv(0)
-    attend(0)
-    for s in (key, value, query):
-        fwd_copy(s, 0).wait_recv()
-        fwd_copy(s, 1).wait_recv()
-        for d in range(1, n_h):
-            hgt_copy(s, 3, d).start()
-        wait_hgt(s, (2, 3))
-        if s == query:
-            project_q(1)
-        else:
-            project_kv(1, s)
+    attend(0, 0, heads)
+    take_fwd(value)
+    wait_hgt(value, (2, 3))
+    project_kv(1, value, False)
+    project_kv(1, value, True)
+    take_fwd(query)
     wait_kv(1)
-    attend(1)
+    attend(1, parity * (heads - early), early)
+    wait_hgt(query, (3,))
+    project_q(1, (1 - parity) * early, heads - early)
+    attend(1, (1 - parity) * early, heads - early)
 
     for s in range(3):
         for i in range(2):
-            own_copy(s, i).wait_send()
+            own_copy(s, 0, i).wait_send()
+            own_copy(s, 1, i).wait_send()
             fwd_copy(s, i).wait_send()
         for piece in range(4):
             for d in range(1, n_h):
@@ -349,7 +395,7 @@
             pltpu.VMEM((2, slots, heads, 3 * count, HEAD_DIM), jnp.bfloat16),
             pltpu.VMEM((2, heads, count, HEAD_DIM), jnp.bfloat16),
             pltpu.VMEM((slots, count, 3 * count), jnp.bfloat16),
-            dma((4,)), dma((2,)), dma((2,)), dma((3, 2)), dma((3, 2)), dma((3, 2)), dma((3, 2)),
+            dma((4,)), dma((2,)), dma((2,)), dma((3, 2, 2)), dma((3, 2, 2)), dma((3, 2)), dma((3, 2)),
             dma((3, 4, n_h - 1)), dma((3, 4, n_h - 1)), dma((2, 2, 2)), dma((2, 2, 2)),
         ],
         compiler_params=pltpu.CompilerParams(

time: 49.1 us -> 46.5 us (0.947)
  Pallas kernels: 47.1 us -> 44.5 us
    pallas_call x1, Pallas kernels: 47.1 us -> 44.5 us  [per_device(): pl.pallas_call(functools.partial(kernel, n_h, n_w), out_shape=jax.ShapeDt...]
where the time goes in v2:
time: 46.5 us; the launch traced here: 46.3 us
  Pallas kernels  44.5 us (96%)
  local copies, waits for them, and re-layouts  1.84 us (4%)
    pallas_call x1, Pallas kernels, per_device(): pl.pallas_call(functools.partial(kernel, n_h, n_w), out_shape=jax.ShapeDt...  44.5 us
    reshape x1, local copies, waits for them, and re-layouts, per_device(): return out.reshape(clips, frames, rows, columns, width)  1.84 us

profile of v2, /device:TPU:0, one launch (start us, length us, event | category | flops | bytes accessed | tf_op | source)
XLA Modules:
  0.0 46.3 jit_solution(18377032130763965905)
XLA Ops:
  0.0 44.5 %shard_map.37 = bf16[256,768]{1,0:T(8,128)(2,1)} custom-call(bf16[1,16,4,4,1536]{4,3,2,1,0:T(4,128)(2,1)} %x_ref.1, bf16[3,96,1536]{2,1,0:T(8,128)(2,1)} %w_ref.1, s32[1,4,2,4]{3,2,1,0:T(2,128)} %tm_ref.1), custom_call_target="tpu_custom_call" | custom-call | tf_op jit(solution)/shard_map/pallas_call | solution.py:381
  44.5 1.8 %reshape.3 = bf16[1,16,4,4,768]{4,3,2,1,0:T(4,128)(2,1)} reshape(bf16[256,768]{1,0:T(8,128)(2,1)} %shard_map.37) | data formatting | bytes 786432 | tf_op jit(solution)/shard_map/reshape | solution.py:405

commit v3 on v2

--- a/solution.py
+++ b/solution.py
@@ -77,9 +77,9 @@
 
     def tok_copy(e):
         target = (f, h, w + 1 if e == 0 else w - 1)
-        return remote(x_ref.at[0], xs.at[0 if e == 0 else 2], tok_s.at[e], tok_r.at[e], target)
-
-    local_x = pltpu.make_async_copy(x_ref.at[0], xs.at[1], loc_sem.at[0])
+        return remote(x_ref.at[0], xs.at[1 if e == 0 else 2], tok_s.at[e], tok_r.at[e], target)
+
+    local_x = pltpu.make_async_copy(x_ref.at[0], xs.at[0], loc_sem.at[0])
     local_w = [
         pltpu.make_async_copy(w_ref.at[s], w_all.at[s, 0, mine], loc_sem.at[1 + s]) for s in range(3)
     ]
@@ -160,7 +160,7 @@
         else:
             row_h = h - 1 if b == 1 else h + 1
         for c in range(3):
-            col_w = w + c - 1
+            col_w = w + (0, -1, 1)[c]
             inside = ((row_h >= 0) & (row_h < total_h) & (col_w >= 0) & (col_w < total_w)).astype(jnp.int32)
             at_h = jnp.minimum(jnp.maximum(row_h, 0), total_h - 1)
             at_w = jnp.minimum(jnp.maximum(col_w, 0), total_w - 1)
@@ -169,7 +169,7 @@
                 flag = tm_ref[0, t, at_h, at_w] * inside
                 flags = jnp.where(k_tile == t, flag, flags)
             seen = flags == 1
-            if b == 0 and c == 1:
+            if b == 0 and c == 0:
                 seen = seen | same
             allowed = jnp.where(near & seen, jnp.float32(1.0), jnp.float32(0.0))
             mask[b, :, c * tokens : (c + 1) * tokens] = allowed.astype(jnp.bfloat16)
@@ -193,22 +193,14 @@
     def project_kv(g, s, sides):
         buf = kbuf if s == key else vbuf
 
-        def block(c):
-            at = pl.ds(pl.multiple_of(c * tokens, tokens), tokens)
-            raw = lax.dot_general(xn[at, :], w_all[s, g], contract_last, preferred_element_type=jnp.float32)
-            for j in range(heads):
-                part = raw[:, j * HEAD_DIM : (j + 1) * HEAD_DIM]
-                buf[g, 0, j, at, :] = head_norm(part) if s == key else part.astype(jnp.bfloat16)
-
+        at = {0: pl.ds(0, tokens), 1: pl.ds(tokens, 2 * tokens), 2: pl.ds(0, 3 * tokens)}[sides]
+        raw = lax.dot_general(xn[at, :], w_all[s, g], contract_last, preferred_element_type=jnp.float32)
+        for j in range(heads):
+            part = raw[:, j * HEAD_DIM : (j + 1) * HEAD_DIM]
+            buf[g, 0, j, at, :] = head_norm(part) if s == key else part.astype(jnp.bfloat16)
         if not sides:
-            block(1)
             return
 
-        def body(i, carry):
-            block(2 * i)
-            return carry
-
-        lax.fori_loop(0, 2, body, 0)
         which = 0 if s == key else 1
 
         @pl.when(has_above)
@@ -222,7 +214,7 @@
     def project_q(g, first, count):
         place = pl.ds(pl.multiple_of(first * HEAD_DIM, HEAD_DIM), count * HEAD_DIM)
         raw = lax.dot_general(
-            xn[tokens : 2 * tokens, :], w_all[query, g, place], contract_last, preferred_element_type=jnp.float32
+            xn[0:tokens, :], w_all[query, g, place], contract_last, preferred_element_type=jnp.float32
         )
         for j in range(count):
             qbuf[g, first + j] = head_norm(raw[:, j * HEAD_DIM : (j + 1) * HEAD_DIM])
@@ -274,7 +266,7 @@
                     vbuf[g, slot] = jnp.zeros(vbuf.shape[2:], jnp.bfloat16)
 
     local_x.wait()
-    normalise(1)
+    normalise(0)
     wait_own(key, 0)
     send_own(value, 0)
     fwd_copy(key, 1).start()
@@ -285,22 +277,22 @@
     send_own(value, 1)
     local_w[key].wait()
     wait_hgt(key, (0, 1))
-    project_kv(0, key, False)
+    project_kv(0, key, 0)
     take_fwd(key)
     send_own(query, 0)
     wait_hgt(key, (2, 3))
-    project_kv(1, key, False)
+    project_kv(1, key, 0)
     wait_own(value, 1)
     send_own(query, 1)
     relay(value, 1, 2)
     @pl.when(has_left)
     def _():
         tok_copy(0).wait_recv()
-        normalise(0)
+        normalise(1)
 
     @pl.when(w == 0)
     def _():
-        blank(0)
+        blank(1)
 
     @pl.when(has_right)
     def _():
@@ -311,17 +303,16 @@
     def _():
         blank(2)
 
-    project_kv(0, key, True)
+    project_kv(0, key, 1)
     wait_own(query, 0)
     send_fwd(value)
     local_w[value].wait()
     wait_hgt(value, (0, 1))
-    project_kv(0, value, False)
-    project_kv(0, value, True)
+    project_kv(0, value, 2)
     wait_own(query, 1)
     send_fwd(query)
     relay(query, 1, 2)
-    project_kv(1, key, True)
+    project_kv(1, key, 1)
     early = n_h * rows // HEAD_DIM
     local_w[query].wait()
     wait_hgt(query, (0, 1))
@@ -332,8 +323,7 @@
     attend(0, 0, heads)
     take_fwd(value)
     wait_hgt(value, (2, 3))
-    project_kv(1, value, False)
-    project_kv(1, value, True)
+    project_kv(1, value, 2)
     take_fwd(query)
     wait_kv(1)
     attend(1, parity * (heads - early), early)

time: 46.5 us -> 45.8 us (0.985)
  Pallas kernels: 44.5 us -> 43.8 us
    pallas_call x1, Pallas kernels: 44.5 us -> 43.8 us  [per_device(): pl.pallas_call(functools.partial(kernel, n_h, n_w), out_shape=jax.ShapeDt...]
where the time goes in v3:
time: 45.8 us; the launch traced here: 45.6 us
  Pallas kernels  43.8 us (96%)
  local copies, waits for them, and re-layouts  1.84 us (4%)
    pallas_call x1, Pallas kernels, per_device(): pl.pallas_call(functools.partial(kernel, n_h, n_w), out_shape=jax.ShapeDt...  43.8 us
    reshape x1, local copies, waits for them, and re-layouts, per_device(): return out.reshape(clips, frames, rows, columns, width)  1.84 us

profile of v3, /device:TPU:0, one launch (start us, length us, event | category | flops | bytes accessed | tf_op | source)
XLA Modules:
  0.0 45.6 jit_solution(2869001638361698882)
XLA Ops:
  0.0 43.8 %shard_map.37 = bf16[256,768]{1,0:T(8,128)(2,1)} custom-call(bf16[1,16,4,4,1536]{4,3,2,1,0:T(4,128)(2,1)} %x_ref.1, bf16[3,96,1536]{2,1,0:T(8,128)(2,1)} %w_ref.1, s32[1,4,2,4]{3,2,1,0:T(2,128)} %tm_ref.1), custom_call_target="tpu_custom_call" | custom-call | tf_op jit(solution)/shard_map/pallas_call | solution.py:371
  43.8 1.8 %reshape.3 = bf16[1,16,4,4,768]{4,3,2,1,0:T(4,128)(2,1)} reshape(bf16[256,768]{1,0:T(8,128)(2,1)} %shard_map.37) | data formatting | bytes 786432 | tf_op jit(solution)/shard_map/reshape | solution.py:395
